TPU v7x, 512 devices: a whole 4x8x8 slice. The times are simulated.
512 devices in a mesh: lon: 16 (over x_hi, y), lat: 32 (over x_lo, z, core).
Axes of the slice: x: 4 (x_hi: 2, x_lo: 2; x = x_hi * 2 + x_lo), y: 8, z: 8, core: 2. Of those that a mesh axis runs over, the one named last changes fastest.
Arguments:
- increment: float32 [64, 256, 4096], P(None, 'lat', 'lon'), may hold values from -6 to 6
- sea_levels: int32 [256, 4096], P('lat', 'lon'), may hold values from 0 to 64, as said below
- cell_sigma: float32 [256, 4096], P('lat', 'lon'), may hold values from 0.3 to 3
- level_sigma: float32 [64], replicated, may hold values from 0.5 to 2
- diffusivity: float32 [64, 256], replicated, may hold values from 0.04 to 0.45
- band_width: int32 [256], replicated, may hold values from 1 to 8, as said below
- vertical_root: float32 [64, 64], replicated
Outputs:
- covariance_product: float32 [64, 256, 4096], P(None, 'lat', 'lon')
Inputs may be any that keep to these rules, and one draw needn't show every extreme that they name: `sea_levels`: some column has 64 sea levels and some are land. `band_width`: some row has half-width 8 and some row 1.
All inputs are finite; a program needn't handle non-finite values.
Results may differ from a plain program's by a relative error of at most 0.00008.
Values sent between devices are 32-bit elements; how exact they have to be, the bound alone decides.
A program may use at most 64 MiB of HBM per device.

v0:
```python
import jax
import jax.numpy as jnp
from jax import lax
from jax.sharding import PartitionSpec as P

WMAX = 8
STEPS = 4


def extended(block, sides, width, periodic):
    for axis, dim in sides:
        count = lax.axis_size(axis)
        forward = [(i, i + 1) for i in range(count - 1)]
        if periodic:
            forward.append((count - 1, 0))
        backward = [(target, source) for source, target in forward]
        low = lax.ppermute(
            lax.slice_in_dim(block, block.shape[dim] - width, None, axis=dim), axis, forward
        )
        high = lax.ppermute(lax.slice_in_dim(block, 0, width, axis=dim), axis, backward)
        block = jnp.concatenate([low, block, high], axis=dim)
    return block


def weights_for(band_rows, offset):
    widths = band_rows.astype(jnp.float32)
    return jnp.maximum(widths + 1.0 - abs(offset), 0.0) / ((widths + 1.0) * (widths + 1.0))


def conv_valid(padded, band_rows):
    count = padded.shape[2] - 2 * WMAX
    total = jnp.zeros((padded.shape[0], padded.shape[1], count), jnp.float32)
    for offset in range(-WMAX, WMAX + 1):
        start = WMAX + offset
        total = (
            total
            + weights_for(band_rows, offset)[None, :, None] * padded[:, :, start : start + count]
        )
    return total


def lon_halo(field):
    return extended(field, (("lon", 2),), WMAX, True)


def zonal_pair(field, band_rows):
    first_pass = conv_valid(lon_halo(field), band_rows)
    result = conv_valid(lon_halo(first_pass), band_rows)
    return result


def meridional(field, faces):
    for step in range(STEPS):
        flux = faces[:, :, None] * (field[:, 1:, :] - field[:, :-1, :])
        edge = jnp.zeros_like(field[:, :1, :])
        field = (
            field + jnp.concatenate([flux, edge], axis=1) - jnp.concatenate([edge, flux], axis=1)
        )
    return field


def rows_diffuse(field, faces):
    rows = field.shape[1]
    wide = extended(field, (("lat", 1),), STEPS, False)
    wide = meridional(wide, faces)
    return wide[:, STEPS : STEPS + rows, :]


def vertical_apply(matrix, field, transposed):
    flat = field.reshape(field.shape[0], -1)
    if transposed:
        result = lax.dot_general(
            matrix,
            flat,
            (((0,), (0,)), ((), ())),
            precision=lax.Precision.HIGHEST,
            preferred_element_type=jnp.float32,
        )
    else:
        result = jnp.dot(
            matrix, flat, precision=lax.Precision.HIGHEST, preferred_element_type=jnp.float32
        )
    return result.reshape(field.shape)


def body(increment, sea_levels, cell_sigma, level_sigma, diffusivity, band_width, vertical_root):
    levels_all = increment.shape[0]
    rows_local = increment.shape[1]
    lat_total = band_width.shape[0]
    lat_index = lax.axis_index("lat")
    levels = lax.broadcasted_iota(jnp.int32, (levels_all, 1, 1), 0)
    sea = (levels < sea_levels[None, :, :]).astype(jnp.float32)
    scale = level_sigma[:, None, None] * cell_sigma[None, :, :]
    field = increment * sea * scale
    field = vertical_apply(vertical_root, field, True)
    columns = lax.broadcasted_iota(jnp.int32, (1, lat_total), 1)
    open_faces = jnp.where(columns < lat_total - 1, diffusivity, 0.0)
    padded_faces = jnp.pad(open_faces, ((0, 0), (STEPS, STEPS)))
    row_start = lat_index * rows_local
    faces = lax.dynamic_slice_in_dim(padded_faces, row_start, rows_local + 2 * STEPS - 1, 1)
    band_rows = lax.dynamic_slice_in_dim(band_width, row_start, rows_local, 0)
    field = rows_diffuse(field, faces)
    field = zonal_pair(field, band_rows)
    field = rows_diffuse(field, faces)
    field = vertical_apply(vertical_root, field, False)
    return field * scale * sea


def solution(mesh):
    return jax.shard_map(
        body,
        mesh=mesh,
        in_specs=(P(None, "lat", "lon"), P("lat", "lon"), P("lat", "lon"), P(), P(), P(), P()),
        out_specs=P(None, "lat", "lon"),
        check_vma=False,
    )
```

profile of v0, /device:TPU:58, one launch (start us, length us, event | category | flops | bytes accessed | tf_op | source)
XLA Modules:
  0.0 76.6 jit_solution(12329490460663511530)
XLA Ops:
  0.0 1.2 %multiply_multiply_fusion.1 = f32[64,8,256]{2,1,0:T(8,128)S(1)} fusion(f32[64,8,256]{2,1,0:T(8,128)} %param.7, f32[8,256]{1,0:T(8,128)} %param.9, f32[64]{0:T(128)} %param.10, s32[8,256]{1,0:T(8,128)} %param.8), kind=kLoop, calls=%fused_computation.82 | loop fusion | flops 524288 | bytes 1065216 | tf_op jit(solution)/shard_map/mul | solution.py:94
  1.2 0.2 copy.8
  1.4 0.6 fusion.106
  2.0 0.2 copy.9
  2.3 1.9 %collective-permute-start = (f32[64,4,256]{2,1,0:T(4,128)S(1)}, f32[64,4,256]{2,1,0:T(4,128)S(1)}, u32[]{:S(2)}, u32[]{:S(2)}) collective-permute-start(f32[64,4,256]{2,1,0:T(4,128)S(1)} %get-tuple-element.13), channel_id=1, source_target_pairs={{0,1},{1,2},{2,3},{3,4},{4,5},{5,6},{6,7},{7,8},{8,9},{9,10},{10,1... | collective-permute-start | bytes 786440 | tf_op jit(solution)/shard_map/ppermute | solution.py:17
  4.2 10.4 %collective-permute-start.1 = (f32[64,4,256]{2,1,0:T(4,128)S(1)}, f32[64,4,256]{2,1,0:T(4,128)S(1)}, u32[]{:S(2)}, u32[]{:S(2)}) collective-permute-start(f32[64,4,256]{2,1,0:T(4,128)S(1)} %get-tuple-element.14), channel_id=1, source_target_pairs={{1,0},{2,1},{3,2},{4,3},{5,4},{6,5},{7,6},{8,7},{9,8},{10,9},{11,1... | collective-permute-start | bytes 786440 | tf_op jit(solution)/shard_map/ppermute | solution.py:20
  14.6 0.7 copy-done.5
  15.5 1.2 %collective-permute-done = f32[64,4,256]{2,1,0:T(4,128)S(1)} collective-permute-done((f32[64,4,256]{2,1,0:T(4,128)S(1)}, f32[64,4,256]{2,1,0:T(4,128)S(1)}, u32[]{:S(2)}, u32[]{:S(2)}) %collective-permute-start) | collective-permute-done | bytes 262176 | tf_op jit(solution)/shard_map/ppermute | solution.py:17
  16.7 1.8 %collective-permute-done.1 = f32[64,4,256]{2,1,0:T(4,128)S(1)} collective-permute-done((f32[64,4,256]{2,1,0:T(4,128)S(1)}, f32[64,4,256]{2,1,0:T(4,128)S(1)}, u32[]{:S(2)}, u32[]{:S(2)}) %collective-permute-start.1) | collective-permute-done | bytes 262176 | tf_op jit(solution)/shard_map/ppermute | solution.py:20
  18.4 0.2 pad_maximum_fusion
  18.6 0.2 fusion.7
  18.9 0.4 pad_subtract_fusion.6
  19.2 0.2 fusion.6
  19.4 0.3 pad_subtract_fusion.5
  19.7 0.2 fusion.5
  19.9 0.3 pad_subtract_fusion.4
  20.2 0.2 fusion.4
  20.4 0.3 pad_subtract_fusion.3
  20.6 0.1 fusion.102
  20.8 3.5 %collective-permute-start.2 = (f32[64,8,8]{2,1,0:T(8,128)S(1)}, f32[64,8,8]{2,1,0:T(8,128)S(1)}, u32[]{:S(2)}, u32[]{:S(2)}) collective-permute-start(f32[64,8,8]{2,1,0:T(8,128)S(1)} %get-tuple-element.7), channel_id=1, source_target_pairs={{0,32},{32,64},{64,96},{96,128},{128,160},{160,192},{192,224},{224... | collective-permute-start | bytes 49160 | tf_op jit(solution)/shard_map/ppermute | solution.py:17
  24.3 2.3 %collective-permute-start.3 = (f32[64,8,8]{2,1,0:T(8,128)S(1)}, f32[64,8,8]{2,1,0:T(8,128)S(1)}, u32[]{:S(2)}, u32[]{:S(2)}) collective-permute-start(f32[64,8,8]{2,1,0:T(8,128)S(1)} %get-tuple-element.8), channel_id=1, source_target_pairs={{32,0},{64,32},{96,64},{128,96},{160,128},{192,160},{224,192},{256... | collective-permute-start | bytes 49160 | tf_op jit(solution)/shard_map/ppermute | solution.py:20
  26.7 2.3 %collective-permute-done.2 = f32[64,8,8]{2,1,0:T(8,128)S(1)} collective-permute-done((f32[64,8,8]{2,1,0:T(8,128)S(1)}, f32[64,8,8]{2,1,0:T(8,128)S(1)}, u32[]{:S(2)}, u32[]{:S(2)}) %collective-permute-start.2) | collective-permute-done | bytes 16416 | tf_op jit(solution)/shard_map/ppermute | solution.py:17
  29.0 7.2 %collective-permute-done.3 = f32[64,8,8]{2,1,0:T(8,128)S(1)} collective-permute-done((f32[64,8,8]{2,1,0:T(8,128)S(1)}, f32[64,8,8]{2,1,0:T(8,128)S(1)}, u32[]{:S(2)}, u32[]{:S(2)}) %collective-permute-start.3) | collective-permute-done | bytes 16416 | tf_op jit(solution)/shard_map/ppermute | solution.py:20
  36.2 3.6 %fusion.56 = f32[64,8,256]{2,1,0:T(8,128)S(1)} fusion(f32[64,8,256]{2,1,0:T(8,128)S(1)} %slice.277, f32[64,8,8]{2,1,0:T(8,128)S(1)} %collective-permute-done.3, f32[64,8,8]{2,1,0:T(8,128)S(1)} %collective-permute-done.2, f32[8]{0:T(128)S(1)} %get-tuple-element.22, f32[8]{0:T(128)S(1)} %get-tuple-element.21, f32[8]{0:T(128)S(1)} %get-tuple-element.20, ...), kind=kLoop, calls=%fused_computation.131 | loop fusion | flops 6422528 | bytes 1081632 | tf_op jit(solution)/shard_map/add | solution.py:36
  39.8 0.1 fusion.104
  40.0 1.9 %collective-permute-start.4 = (f32[64,8,8]{2,1,0:T(8,128)S(1)}, f32[64,8,8]{2,1,0:T(8,128)S(1)}, u32[]{:S(2)}, u32[]{:S(2)}) collective-permute-start(f32[64,8,8]{2,1,0:T(8,128)S(1)} %get-tuple-element.11), channel_id=1, source_target_pairs={{0,32},{32,64},{64,96},{96,128},{128,160},{160,192},{192,224},{224... | collective-permute-start | bytes 49160 | tf_op jit(solution)/shard_map/ppermute | solution.py:17
  41.9 3.9 %collective-permute-start.5 = (f32[64,8,8]{2,1,0:T(8,128)S(1)}, f32[64,8,8]{2,1,0:T(8,128)S(1)}, u32[]{:S(2)}, u32[]{:S(2)}) collective-permute-start(f32[64,8,8]{2,1,0:T(8,128)S(1)} %get-tuple-element.12), channel_id=1, source_target_pairs={{32,0},{64,32},{96,64},{128,96},{160,128},{192,160},{224,192},{256... | collective-permute-start | bytes 49160 | tf_op jit(solution)/shard_map/ppermute | solution.py:20
  45.8 2.4 %collective-permute-done.4 = f32[64,8,8]{2,1,0:T(8,128)S(1)} collective-permute-done((f32[64,8,8]{2,1,0:T(8,128)S(1)}, f32[64,8,8]{2,1,0:T(8,128)S(1)}, u32[]{:S(2)}, u32[]{:S(2)}) %collective-permute-start.4) | collective-permute-done | bytes 16416 | tf_op jit(solution)/shard_map/ppermute | solution.py:17
  48.2 5.5 %collective-permute-done.5 = f32[64,8,8]{2,1,0:T(8,128)S(1)} collective-permute-done((f32[64,8,8]{2,1,0:T(8,128)S(1)}, f32[64,8,8]{2,1,0:T(8,128)S(1)}, u32[]{:S(2)}, u32[]{:S(2)}) %collective-permute-start.5) | collective-permute-done | bytes 16416 | tf_op jit(solution)/shard_map/ppermute | solution.py:20
  53.8 3.6 %fusion.12 = f32[64,8,256]{2,1,0:T(8,128)S(1)} fusion(f32[64,8,256]{2,1,0:T(8,128)S(1)} %fusion.56, f32[64,8,8]{2,1,0:T(8,128)S(1)} %collective-permute-done.5, f32[64,8,8]{2,1,0:T(8,128)S(1)} %collective-permute-done.4, f32[8]{0:T(128)S(1)} %get-tuple-element.22, f32[8]{0:T(128)S(1)} %get-tuple-element.21, f32[8]{0:T(128)S(1)} %get-tuple-element.20, ...), kind=kLoop, calls=%fused_computation.87 | loop fusion | flops 6422528 | bytes 1081632 | tf_op jit(solution)/shard_map/add | solution.py:36
  57.5 1.9 %collective-permute-start.6 = (f32[64,4,256]{2,1,0:T(4,128)S(1)}, f32[64,4,256]{2,1,0:T(4,128)S(1)}, u32[]{:S(2)}, u32[]{:S(2)}) collective-permute-start(f32[64,4,256]{2,1,0:T(4,128)S(1)} %get-tuple-element.9), channel_id=1, source_target_pairs={{0,1},{1,2},{2,3},{3,4},{4,5},{5,6},{6,7},{7,8},{8,9},{9,10},{10,1... | collective-permute-start | bytes 786440 | tf_op jit(solution)/shard_map/ppermute | solution.py:17
  59.4 8.7 %collective-permute-start.7 = (f32[64,4,256]{2,1,0:T(4,128)S(1)}, f32[64,4,256]{2,1,0:T(4,128)S(1)}, u32[]{:S(2)}, u32[]{:S(2)}) collective-permute-start(f32[64,4,256]{2,1,0:T(4,128)S(1)} %get-tuple-element.10), channel_id=1, source_target_pairs={{1,0},{2,1},{3,2},{4,3},{5,4},{6,5},{7,6},{8,7},{9,8},{10,9},{11,1... | collective-permute-start | bytes 786440 | tf_op jit(solution)/shard_map/ppermute | solution.py:20
  68.1 2.1 %collective-permute-done.6 = f32[64,4,256]{2,1,0:T(4,128)S(1)} collective-permute-done((f32[64,4,256]{2,1,0:T(4,128)S(1)}, f32[64,4,256]{2,1,0:T(4,128)S(1)}, u32[]{:S(2)}, u32[]{:S(2)}) %collective-permute-start.6) | collective-permute-done | bytes 262176 | tf_op jit(solution)/shard_map/ppermute | solution.py:17
  70.2 1.8 %collective-permute-done.7 = f32[64,4,256]{2,1,0:T(4,128)S(1)} collective-permute-done((f32[64,4,256]{2,1,0:T(4,128)S(1)}, f32[64,4,256]{2,1,0:T(4,128)S(1)}, u32[]{:S(2)}, u32[]{:S(2)}) %collective-permute-start.7) | collective-permute-done | bytes 262176 | tf_op jit(solution)/shard_map/ppermute | solution.py:20
  72.0 0.2 pad_maximum_fusion.1
  72.2 0.2 fusion.3
  72.4 0.4 pad_subtract_fusion.2
  72.8 0.2 fusion.2
  73.0 0.3 pad_subtract_fusion.1
  73.3 0.2 fusion.1
  73.5 0.3 pad_subtract_fusion
  73.7 0.2 fusion
  74.0 0.2 pad_subtract_fusion.7
  74.1 0.2 copy.10
  74.3 0.6 fusion.107
  75.0 0.2 copy.11
  75.1 0.5 copy-done.2
  75.6 0.9 %fusion.8 = f32[64,8,256]{2,1,0:T(8,128)} fusion(f32[8,8,8,256]{3,2,1,0:T(8,128)S(1)} %copy.11, f32[8,256]{1,0:T(8,128)S(1)} %copy-done.2, f32[64]{0:T(128)S(1)} %copy-done.4, s32[8,256]{1,0:T(8,128)S(1)} %copy-done.3), kind=kLoop, calls=%fused_computation.83 | loop fusion | flops 524288 | bytes 1065216 | tf_op jit(solution)/shard_map/mul | solution.py:106
  (18 shorter events, 0.5 us)
Async XLA Ops:
  0.0 1.4 %copy-start = (f32[64,64]{1,0:T(8,128)S(1)}, f32[64,64]{1,0:T(8,128)}, u32[]{:S(2)}) copy-start(f32[64,64]{1,0:T(8,128)} %param.13) | copy-start | bytes 49156
  2.2 12.4 %copy-start.1 = (f32[64,256]{1,0:T(8,128)S(1)}, f32[64,256]{1,0:T(8,128)}, u32[]{:S(2)}) copy-start(f32[64,256]{1,0:T(8,128)} %param.11) | copy-start | bytes 196612
  2.3 14.4 %collective-permute-start = (f32[64,4,256]{2,1,0:T(4,128)S(1)}, f32[64,4,256]{2,1,0:T(4,128)S(1)}, u32[]{:S(2)}, u32[]{:S(2)}) collective-permute-start(f32[64,4,256]{2,1,0:T(4,128)S(1)} %get-tuple-element.13), channel_id=1, source_target_pairs={{0,1},{1,2},{2,3},{3,4},{4,5},{5,6},{6,7},{7,8},{8,9},{9,10},{10,1... | collective-permute-start | bytes 786440 | tf_op jit(solution)/shard_map/ppermute | solution.py:17
  4.2 14.2 %collective-permute-start.1 = (f32[64,4,256]{2,1,0:T(4,128)S(1)}, f32[64,4,256]{2,1,0:T(4,128)S(1)}, u32[]{:S(2)}, u32[]{:S(2)}) collective-permute-start(f32[64,4,256]{2,1,0:T(4,128)S(1)} %get-tuple-element.14), channel_id=1, source_target_pairs={{1,0},{2,1},{3,2},{4,3},{5,4},{6,5},{7,6},{8,7},{9,8},{10,9},{11,1... | collective-permute-start | bytes 786440 | tf_op jit(solution)/shard_map/ppermute | solution.py:20
  14.6 0.7 copy-start.5
  20.8 8.3 %collective-permute-start.2 = (f32[64,8,8]{2,1,0:T(8,128)S(1)}, f32[64,8,8]{2,1,0:T(8,128)S(1)}, u32[]{:S(2)}, u32[]{:S(2)}) collective-permute-start(f32[64,8,8]{2,1,0:T(8,128)S(1)} %get-tuple-element.7), channel_id=1, source_target_pairs={{0,32},{32,64},{64,96},{96,128},{128,160},{160,192},{192,224},{224... | collective-permute-start | bytes 49160 | tf_op jit(solution)/shard_map/ppermute | solution.py:17
  24.3 11.9 %collective-permute-start.3 = (f32[64,8,8]{2,1,0:T(8,128)S(1)}, f32[64,8,8]{2,1,0:T(8,128)S(1)}, u32[]{:S(2)}, u32[]{:S(2)}) collective-permute-start(f32[64,8,8]{2,1,0:T(8,128)S(1)} %get-tuple-element.8), channel_id=1, source_target_pairs={{32,0},{64,32},{96,64},{128,96},{160,128},{192,160},{224,192},{256... | collective-permute-start | bytes 49160 | tf_op jit(solution)/shard_map/ppermute | solution.py:20
  40.0 8.3 %collective-permute-start.4 = (f32[64,8,8]{2,1,0:T(8,128)S(1)}, f32[64,8,8]{2,1,0:T(8,128)S(1)}, u32[]{:S(2)}, u32[]{:S(2)}) collective-permute-start(f32[64,8,8]{2,1,0:T(8,128)S(1)} %get-tuple-element.11), channel_id=1, source_target_pairs={{0,32},{32,64},{64,96},{96,128},{128,160},{160,192},{192,224},{224... | collective-permute-start | bytes 49160 | tf_op jit(solution)/shard_map/ppermute | solution.py:17
  41.9 11.9 %collective-permute-start.5 = (f32[64,8,8]{2,1,0:T(8,128)S(1)}, f32[64,8,8]{2,1,0:T(8,128)S(1)}, u32[]{:S(2)}, u32[]{:S(2)}) collective-permute-start(f32[64,8,8]{2,1,0:T(8,128)S(1)} %get-tuple-element.12), channel_id=1, source_target_pairs={{32,0},{64,32},{96,64},{128,96},{160,128},{192,160},{224,192},{256... | collective-permute-start | bytes 49160 | tf_op jit(solution)/shard_map/ppermute | solution.py:20
  57.5 12.8 %collective-permute-start.6 = (f32[64,4,256]{2,1,0:T(4,128)S(1)}, f32[64,4,256]{2,1,0:T(4,128)S(1)}, u32[]{:S(2)}, u32[]{:S(2)}) collective-permute-start(f32[64,4,256]{2,1,0:T(4,128)S(1)} %get-tuple-element.9), channel_id=1, source_target_pairs={{0,1},{1,2},{2,3},{3,4},{4,5},{5,6},{6,7},{7,8},{8,9},{9,10},{10,1... | collective-permute-start | bytes 786440 | tf_op jit(solution)/shard_map/ppermute | solution.py:17
  59.4 12.6 %collective-permute-start.7 = (f32[64,4,256]{2,1,0:T(4,128)S(1)}, f32[64,4,256]{2,1,0:T(4,128)S(1)}, u32[]{:S(2)}, u32[]{:S(2)}) collective-permute-start(f32[64,4,256]{2,1,0:T(4,128)S(1)} %get-tuple-element.10), channel_id=1, source_target_pairs={{1,0},{2,1},{3,2},{4,3},{5,4},{6,5},{7,6},{8,7},{9,8},{10,9},{11,1... | collective-permute-start | bytes 786440 | tf_op jit(solution)/shard_map/ppermute | solution.py:20
  74.9 0.7 copy-start.2
  74.9 0.7 copy-start.3
  74.9 0.7 copy-start.4
where the time goes:
time: 77 us; the launch traced here: 76.6 us
  starting transfers between devices  34.6 us (45%)
  waiting for transfers between devices  24.3 us (32%)
  other arithmetic  13.7 us (18%)
  local copies, waits for them, and re-layouts  2.43 us (3%)
  matrix products  1.23 us (2%)
    ppermute x4, starting transfers between devices, extended(): lax.ppermute(lax.slice_in_dim(block, 0, width, axis=dim), axis, backward)  25.3 us
    ppermute x4, waiting for transfers between devices, extended(): lax.ppermute(lax.slice_in_dim(block, 0, width, axis=dim), axis, backward)  16.2 us
    ppermute x4, starting transfers between devices, extended(): lax.ppermute(lax.slice_in_dim(block, block.shape[dim] - width, None, axis...  9.3 us
    ppermute x4, waiting for transfers between devices, extended(): lax.ppermute(lax.slice_in_dim(block, block.shape[dim] - width, None, axis...  8.06 us
    add x2, other arithmetic, conv_valid(): total + weights_for(band_rows, offset)[None, :, None] * padded[:, :, star...  7.23 us
    sub x8, other arithmetic, meridional(): field + jnp.concatenate([flux, edge], axis=1)  2.16 us
    unnamed x16, local copies, waits for them, and re-layouts  1.86 us
    mul x8, other arithmetic, meridional(): flux = faces[:, :, None] * (field[:, 1:, :] - field[:, :-1, :])  1.65 us
  transfers between devices with their start and end apart: 8, of which 8 were waited for; matrix products, arithmetic and copies ran while one was open for 0% of the time, Pallas kernels for 0%

commit v1 on v0

v1 whole, which is shorter than its diff:
```python
import functools

import jax
import jax.numpy as jnp
from jax import lax
from jax.experimental import pallas as pl
from jax.experimental.pallas import tpu as pltpu
from jax.sharding import PartitionSpec as P

STEPS = 4
HALO = 16
CHUNKS = 2
F32 = jnp.float32
BF16 = jnp.bfloat16
MESH = pl.DeviceIdType.MESH


def split(value):
    high = value.astype(BF16)
    return high, (value - high.astype(F32)).astype(BF16)


def dot(left, right):
    return jnp.dot(left, right, preferred_element_type=F32)


def band(distance, width):
    u = jnp.maximum(2.0 * width - 1.0 - jnp.abs(distance), 0.0)
    v = jnp.maximum(u - width, 0.0)
    return u * (u + 1.0) * (u + 2.0) - 4.0 * (v * (v + 1.0) * (v + 2.0))


def diffuse(rows, faces):
    for step in range(STEPS):
        flux = [faces[step + m] * (rows[m + 1] - rows[m]) for m in range(len(rows) - 1)]
        rows = [rows[m] + (flux[m] - flux[m - 1]) for m in range(1, len(rows) - 1)]
    return rows


def kernel(
    band_ref, inc_hbm, sea_ref, cell_ref, sigma_ref, diff_ref, root_ref, out_hbm,
    inc_ref, out_ref, first, second, mid, fin, edge, halo, faces_ref, w_high, w_low, zscale,
    load_sem, send_edge, recv_edge, send_lat, recv_lat,
):
    nz = root_ref.shape[0]
    lat_total = diff_ref.shape[1]
    part = nz // CHUNKS
    lat_count, lon_count = lax.axis_size("lat"), lax.axis_size("lon")
    lat, lon = lax.axis_index("lat"), lax.axis_index("lon")
    north, south = lax.rem(lat + 1, lat_count), lax.rem(lat + lat_count - 1, lat_count)
    east, west = lax.rem(lon + 1, lon_count), lax.rem(lon + lon_count - 1, lon_count)

    loads = [
        pltpu.make_async_copy(inc_hbm.at[:, pl.ds(128 * h, 128)], inc_ref.at[h], load_sem.at[h])
        for h in range(2)
    ]
    for load in loads:
        load.start()
    barrier = pltpu.get_barrier_semaphore()
    for a, o in (
        (north, lon), (south, lon), (lat, east), (lat, west),
        (north, east), (north, west), (south, east), (south, west),
    ):
        pl.semaphore_signal(barrier, inc=1, device_id={"lat": a, "lon": o}, device_id_type=MESH)

    lift = root_ref[...].T * sigma_ref[...]
    lift_high, lift_low = split(lift)
    lift3 = jnp.concatenate([lift_high, lift_high, lift_low], axis=1)
    lower_high, lower_low = split(lift.T)
    lower3 = jnp.concatenate([lower_high, lower_high, lower_low], axis=1)

    level = lax.broadcasted_iota(jnp.int32, (nz, 256), 0)
    lane128 = lax.broadcasted_iota(jnp.int32, (nz, 128), 1)

    for load in loads:
        load.wait()
    left_pack = jnp.zeros((nz, 128), F32)
    right_pack = jnp.zeros((nz, 128), F32)
    for j in range(8):
        sea = level < sea_ref[j : j + 1, :]
        raw = jnp.concatenate([inc_ref[h, pl.ds(j, nz, stride=8), :] for h in range(2)], axis=1)
        start = jnp.where(sea, raw * cell_ref[j : j + 1, :], 0.0)
        high, low = split(start)
        lifted = dot(lift3, jnp.concatenate([high, low, high], axis=0))
        for c in range(CHUNKS):
            first[c, 4 + j] = lifted[c * part : (c + 1) * part]
        mine = (lane128 >= HALO * j) & (lane128 < HALO * (j + 1))
        left = pltpu.roll(lifted[:, :128], HALO * j, 1) if j else lifted[:, :128]
        shift = (HALO * j - 112) % 128
        right = pltpu.roll(lifted[:, 128:], shift, 1) if shift else lifted[:, 128:]
        left_pack = jnp.where(mine, left, left_pack)
        right_pack = jnp.where(mine, right, right_pack)
    edge[0] = left_pack
    edge[1] = right_pack

    pl.semaphore_wait(barrier, 8)
    edge_copies = []
    for side, o in ((0, west), (1, east)):
        for slot, a in ((0, lat), (1, south), (2, north)):
            copy = pltpu.make_async_remote_copy(
                src_ref=edge.at[side],
                dst_ref=halo.at[1 - side, slot],
                send_sem=send_edge.at[side, slot],
                recv_sem=recv_edge.at[1 - side, slot],
                device_id={"lat": a, "lon": o},
                device_id_type=MESH,
            )
            copy.start()
            edge_copies.append(copy)

    def lat_copies(buffer, turn, c):
        copies = []
        for way, source, target, a in ((0, 4, 12, south), (1, 8, 0, north)):
            copy = pltpu.make_async_remote_copy(
                src_ref=buffer.at[c, pl.ds(source, 4)],
                dst_ref=buffer.at[c, pl.ds(target, 4)],
                send_sem=send_lat.at[turn, c, way],
                recv_sem=recv_lat.at[turn, c, way],
                device_id={"lat": a, "lon": lon},
                device_id_type=MESH,
            )
            copy.start()
            copies.append(copy)
        return copies

    first_copies = [lat_copies(first, 0, c) for c in range(CHUNKS)]

    column = lax.broadcasted_iota(jnp.int32, (lat_total, 256), 0)
    block = lax.broadcasted_iota(jnp.int32, (lat_total, 256), 1) // HALO
    row = 8 * lat + jnp.where(block < 12, block, block - 16)
    pick = jnp.where((column == row) & (column < lat_total - 1), 1.0, 0.0).astype(BF16)
    d_high, rest = diff_ref[...].astype(BF16), None
    rest = diff_ref[...] - d_high.astype(F32)
    d_mid, d_low = split(rest)
    packed_faces = dot(d_high, pick) + dot(d_mid, pick) + dot(d_low, pick)
    for m in range(15):
        lane = HALO * ((m - 4) % 16)
        faces_ref[m] = jnp.broadcast_to(packed_faces[:, lane : lane + 1], (nz, 128))

    inner = (
        lax.broadcasted_iota(jnp.int32, (128, 128), 0) - lax.broadcasted_iota(jnp.int32, (128, 128), 1)
    ).astype(F32)
    outer = (
        lax.broadcasted_iota(jnp.int32, (HALO, 128), 0) - lax.broadcasted_iota(jnp.int32, (HALO, 128), 1)
    ).astype(F32)
    w_high[...] = jnp.zeros_like(w_high)
    w_low[...] = jnp.zeros_like(w_low)
    for j in range(8):
        width = band_ref[8 * lat + j].astype(F32) + 1.0
        zscale[j : j + 1, :] = 1.0 / jnp.full((1, 256), 6.0 * (width * width) * (width * width), F32)
        for ref, a, b, c in zip(
            (w_high, w_low),
            split(band(inner, width)),
            split(band(outer - 16.0, width)),
            split(band(outer + 128.0, width)),
        ):
            ref[j, 0:128, 0:128] = a
            ref[j, 128:256, 128:256] = a
            ref[j, 112:128, 128:256] = b
            ref[j, 256 + HALO * j : 272 + HALO * j, 0:128] = b
            ref[j, 128:144, 0:128] = c
            ref[j, 384 + HALO * j : 400 + HALO * j, 128:256] = c

    for copy in edge_copies:
        copy.wait_recv()
    sides = []
    for side in range(2):
        other = jnp.where(lane128 < 64, halo[side, 1], halo[side, 2])
        field = jnp.concatenate([halo[side, 0], other], axis=1)
        for step in range(STEPS):
            flux = packed_faces * (pltpu.roll(field, 256 - HALO, 1) - field)
            field = field + (flux - pltpu.roll(flux, HALO, 1))
        sides.append(field[:, :128])
    halo_high, halo_low = split(jnp.concatenate(sides, axis=1))

    def rows_pass(buffer, c, store):
        def group(g, carry):
            at = pl.multiple_of(g * 8, 8)
            whole = pl.multiple_of(c * part + g * 8, 8)
            faces = [faces_ref[m, pl.ds(whole, 8), :] for m in range(15)]
            for half in range(2):
                lanes = slice(128 * half, 128 * half + 128)
                rows = [buffer[c, m, pl.ds(at, 8), lanes] for m in range(16)]
                for j, value in enumerate(diffuse(rows, faces)):
                    store[j, pl.ds(whole, 8), lanes] = value
            return carry

        lax.fori_loop(0, part // 8, group, 0)

    second_copies = []
    for c in range(CHUNKS):
        for copy in first_copies[c]:
            copy.wait_recv()
        rows_pass(first, c, mid)
        levels = slice(c * part, (c + 1) * part)
        for j in range(8):
            high, low = split(mid[j, levels, :])
            high = jnp.concatenate([high, halo_high[levels]], axis=1)
            low = jnp.concatenate([low, halo_low[levels]], axis=1)
            both = dot(jnp.concatenate([high, low], axis=0), w_high[j])
            total = both[:part] + both[part:] + dot(high, w_low[j])
            second[c, 4 + j] = total * zscale[j : j + 1, :]
        second_copies.append(lat_copies(second, 1, c))

    for c in range(CHUNKS):
        for copy in second_copies[c]:
            copy.wait_recv()
        rows_pass(second, c, fin)

    for j in range(8):
        high, low = split(fin[j])
        lowered = dot(lower3, jnp.concatenate([high, low, high], axis=0))
        sea = level < sea_ref[j : j + 1, :]
        result = jnp.where(sea, lowered * cell_ref[j : j + 1, :], 0.0)
        for h in range(2):
            out_ref[h, pl.ds(j, nz, stride=8), :] = result[:, 128 * h : 128 * h + 128]
    stores = [
        pltpu.make_async_copy(out_ref.at[h], out_hbm.at[:, pl.ds(128 * h, 128)], load_sem.at[h])
        for h in range(2)
    ]
    for store in stores:
        store.start()
    for copy in edge_copies:
        copy.wait_send()
    for group in first_copies + second_copies:
        for copy in group:
            copy.wait_send()
    for store in stores:
        store.wait()


def body(increment, sea_levels, cell_sigma, level_sigma, diffusivity, band_width, vertical_root):
    nz, rows, columns = increment.shape
    part = nz // CHUNKS
    vmem = pl.BlockSpec(memory_space=pltpu.VMEM)
    result = pl.pallas_call(
        kernel,
        out_shape=jax.ShapeDtypeStruct((nz * rows, columns), F32),
        in_specs=[
            pl.BlockSpec(memory_space=pltpu.SMEM),
            pl.BlockSpec(memory_space=pl.ANY),
            vmem, vmem, vmem, vmem, vmem,
        ],
        out_specs=pl.BlockSpec(memory_space=pl.ANY),
        scratch_shapes=[
            pltpu.VMEM((2, nz * rows, 128), F32),
            pltpu.VMEM((2, nz * rows, 128), F32),
            pltpu.VMEM((CHUNKS, 16, part, columns), F32),
            pltpu.VMEM((CHUNKS, 16, part, columns), F32),
            pltpu.VMEM((8, nz, columns), F32),
            pltpu.VMEM((8, nz, columns), F32),
            pltpu.VMEM((2, nz, 128), F32),
            pltpu.VMEM((2, 3, nz, 128), F32),
            pltpu.VMEM((15, nz, 128), F32),
            pltpu.VMEM((8, 512, 256), BF16),
            pltpu.VMEM((8, 512, 256), BF16),
            pltpu.VMEM((8, 256), F32),
            pltpu.SemaphoreType.DMA((2,)),
            pltpu.SemaphoreType.DMA((2, 3)),
            pltpu.SemaphoreType.DMA((2, 3)),
            pltpu.SemaphoreType.DMA((2, CHUNKS, 2)),
            pltpu.SemaphoreType.DMA((2, CHUNKS, 2)),
        ],
        compiler_params=pltpu.CompilerParams(collective_id=0, has_side_effects=True),
        name="covariance",
    )(
        band_width,
        increment.reshape(nz * rows, columns),
        sea_levels,
        cell_sigma,
        level_sigma.reshape(1, nz),
        diffusivity,
        vertical_root,
    )
    return result.reshape(nz, rows, columns)


def solution(mesh):
    return jax.shard_map(
        body,
        mesh=mesh,
        in_specs=(P(None, "lat", "lon"), P("lat", "lon"), P("lat", "lon"), P(), P(), P(), P()),
        out_specs=P(None, "lat", "lon"),
        check_vma=False,
    )
```

time: 77 us -> 30.9 us (0.40)
  the two profiles are of different devices: /device:TPU:58 before, /device:TPU:2 now
where the time goes in v1:
time: 30.9 us; the launch traced here: 30.6 us
  Pallas kernels  28.8 us (93%)
  local copies, waits for them, and re-layouts  1.87 us (6%)
    pallas_call x1, Pallas kernels, body(): pl.pallas_call(kernel, out_shape=jax.ShapeDtypeStruct((nz * rows, columns...  28.8 us
    unnamed x1, local copies, waits for them, and re-layouts  1.87 us

profile of v1, /device:TPU:2, one launch (start us, length us, event | category | flops | bytes accessed | tf_op | source)
XLA Modules:
  0.0 30.6 jit_solution(8779513953509149677)
XLA Ops:
  0.0 28.8 %covariance.1 = f32[512,256]{1,0:T(8,128)} custom-call(s32[256]{0:T(256)} %band_ref.1, f32[512,256]{1,0:T(8,128)} %bitcast.4, s32[8,256]{1,0:T(8,128)} %sea_ref.1, f32[8,256]{1,0:T(8,128)} %cell_ref.1, f32[1,64]{1,0:T(1,128)} %bitcast.5, f32[64,256]{1,0:T(8,128)} %diff_ref.1, f32[64,64]{1,0:T(8,128)} %root_ref.1), custom_call_target="tpu_custom_call" | custom-call | tf_op jit(solution)/shard_map/covariance/pallas_call | solution.py:236
  28.8 1.9 %copy.9 = f32[64,8,256]{2,1,0:T(8,128)} copy(f32[64,8,256]{2,1,0:T(8,128)} %bitcast.3) | data formatting | bytes 1048576

commit v2 on v1

--- a/solution.py
+++ b/solution.py
@@ -38,9 +38,10 @@
 
 
 def kernel(
-    band_ref, inc_hbm, sea_ref, cell_ref, sigma_ref, diff_ref, root_ref, out_hbm,
-    inc_ref, out_ref, first, second, mid, fin, edge, halo, faces_ref, w_high, w_low, zscale,
-    load_sem, send_edge, recv_edge, send_lat, recv_lat,
+    band_hbm, inc_hbm, sea_hbm, cell_hbm, sigma_hbm, diff_hbm, root_hbm, out_ref,
+    band_ref, sea_ref, cell_ref, sigma_ref, diff_ref, root_ref,
+    inc_ref, first, second, mid, fin, edge, corner, halo, other, faces_ref, w_high, w_low, zscale,
+    load_sem, send_edge, recv_edge, send_corner, recv_corner, send_lat, recv_lat,
 ):
     nz = root_ref.shape[0]
     lat_total = diff_ref.shape[1]
@@ -54,6 +55,13 @@
         pltpu.make_async_copy(inc_hbm.at[:, pl.ds(128 * h, 128)], inc_ref.at[h], load_sem.at[h])
         for h in range(2)
     ]
+    for i, (source, target) in enumerate(
+        (
+            (root_hbm, root_ref), (sigma_hbm, sigma_ref), (sea_hbm, sea_ref), (cell_hbm, cell_ref),
+            (diff_hbm, diff_ref), (band_hbm, band_ref),
+        )
+    ):
+        loads.append(pltpu.make_async_copy(source, target, load_sem.at[2 + i]))
     for load in loads:
         load.start()
     barrier = pltpu.get_barrier_semaphore()
@@ -63,6 +71,8 @@
     ):
         pl.semaphore_signal(barrier, inc=1, device_id={"lat": a, "lon": o}, device_id_type=MESH)
 
+    loads[2].wait()
+    loads[3].wait()
     lift = root_ref[...].T * sigma_ref[...]
     lift_high, lift_low = split(lift)
     lift3 = jnp.concatenate([lift_high, lift_high, lift_low], axis=1)
@@ -72,7 +82,7 @@
     level = lax.broadcasted_iota(jnp.int32, (nz, 256), 0)
     lane128 = lax.broadcasted_iota(jnp.int32, (nz, 128), 1)
 
-    for load in loads:
+    for load in loads[4:6] + loads[:2]:
         load.wait()
     left_pack = jnp.zeros((nz, 128), F32)
     right_pack = jnp.zeros((nz, 128), F32)
@@ -90,23 +100,12 @@
         right = pltpu.roll(lifted[:, 128:], shift, 1) if shift else lifted[:, 128:]
         left_pack = jnp.where(mine, left, left_pack)
         right_pack = jnp.where(mine, right, right_pack)
-    edge[0] = left_pack
-    edge[1] = right_pack
-
-    pl.semaphore_wait(barrier, 8)
-    edge_copies = []
-    for side, o in ((0, west), (1, east)):
-        for slot, a in ((0, lat), (1, south), (2, north)):
-            copy = pltpu.make_async_remote_copy(
-                src_ref=edge.at[side],
-                dst_ref=halo.at[1 - side, slot],
-                send_sem=send_edge.at[side, slot],
-                recv_sem=recv_edge.at[1 - side, slot],
-                device_id={"lat": a, "lon": o},
-                device_id_type=MESH,
-            )
-            copy.start()
-            edge_copies.append(copy)
+    low_lanes = lane128[: nz // 2] < 64
+    for side, pack in enumerate((left_pack, right_pack)):
+        edge[side] = pack
+        upper, turned = pack[: nz // 2], pltpu.roll(pack[nz // 2 :], 64, 1)
+        corner[side, 0] = jnp.where(low_lanes, upper, turned)
+        corner[side, 1] = jnp.where(low_lanes, turned, upper)
 
     def lat_copies(buffer, turn, c):
         copies = []
@@ -123,8 +122,36 @@
             copies.append(copy)
         return copies
 
-    first_copies = [lat_copies(first, 0, c) for c in range(CHUNKS)]
-
+    pl.semaphore_wait(barrier, 8)
+    edge_copies = []
+    for side, o in ((0, west), (1, east)):
+        copy = pltpu.make_async_remote_copy(
+            src_ref=edge.at[side],
+            dst_ref=halo.at[1 - side],
+            send_sem=send_edge.at[side],
+            recv_sem=recv_edge.at[1 - side],
+            device_id={"lat": lat, "lon": o},
+            device_id_type=MESH,
+        )
+        copy.start()
+        edge_copies.append(copy)
+    first_copies = [lat_copies(first, 0, 0)]
+    for side, o in ((0, west), (1, east)):
+        for way, a in ((0, south), (1, north)):
+            copy = pltpu.make_async_remote_copy(
+                src_ref=corner.at[side, way],
+                dst_ref=other.at[1 - side, way],
+                send_sem=send_corner.at[side, way],
+                recv_sem=recv_corner.at[1 - side, way],
+                device_id={"lat": a, "lon": o},
+                device_id_type=MESH,
+            )
+            copy.start()
+            edge_copies.append(copy)
+    first_copies += [lat_copies(first, 0, c) for c in range(1, CHUNKS)]
+
+    for load in loads[6:]:
+        load.wait()
     column = lax.broadcasted_iota(jnp.int32, (lat_total, 256), 0)
     block = lax.broadcasted_iota(jnp.int32, (lat_total, 256), 1) // HALO
     row = 8 * lat + jnp.where(block < 12, block, block - 16)
@@ -161,17 +188,25 @@
             ref[j, 128:144, 0:128] = c
             ref[j, 384 + HALO * j : 400 + HALO * j, 128:256] = c
 
-    for copy in edge_copies:
-        copy.wait_recv()
-    sides = []
-    for side in range(2):
-        other = jnp.where(lane128 < 64, halo[side, 1], halo[side, 2])
-        field = jnp.concatenate([halo[side, 0], other], axis=1)
-        for step in range(STEPS):
-            flux = packed_faces * (pltpu.roll(field, 256 - HALO, 1) - field)
-            field = field + (flux - pltpu.roll(flux, HALO, 1))
-        sides.append(field[:, :128])
-    halo_high, halo_low = split(jnp.concatenate(sides, axis=1))
+    def halo_pass():
+        for copy in edge_copies:
+            copy.wait_recv()
+        sides = []
+        for side in range(2):
+            above, below = other[side, 0], other[side, 1]
+            far = jnp.concatenate(
+                [
+                    jnp.where(low_lanes, above, below),
+                    pltpu.roll(jnp.where(low_lanes, below, above), 64, 1),
+                ],
+                axis=0,
+            )
+            field = jnp.concatenate([halo[side], far], axis=1)
+            for step in range(STEPS):
+                flux = packed_faces * (pltpu.roll(field, 256 - HALO, 1) - field)
+                field = field + (flux - pltpu.roll(flux, HALO, 1))
+            sides.append(field[:, :128])
+        return split(jnp.concatenate(sides, axis=1))
 
     def rows_pass(buffer, c, store):
         def group(g, carry):
@@ -192,6 +227,8 @@
         for copy in first_copies[c]:
             copy.wait_recv()
         rows_pass(first, c, mid)
+        if c == 0:
+            halo_high, halo_low = halo_pass()
         levels = slice(c * part, (c + 1) * part)
         for j in range(8):
             high, low = split(mid[j, levels, :])
@@ -213,57 +250,56 @@
         sea = level < sea_ref[j : j + 1, :]
         result = jnp.where(sea, lowered * cell_ref[j : j + 1, :], 0.0)
         for h in range(2):
-            out_ref[h, pl.ds(j, nz, stride=8), :] = result[:, 128 * h : 128 * h + 128]
-    stores = [
-        pltpu.make_async_copy(out_ref.at[h], out_hbm.at[:, pl.ds(128 * h, 128)], load_sem.at[h])
-        for h in range(2)
-    ]
-    for store in stores:
-        store.start()
+            out_ref[pl.ds(8 * h + j, nz, stride=16), :] = result[:, 128 * h : 128 * h + 128]
     for copy in edge_copies:
         copy.wait_send()
     for group in first_copies + second_copies:
         for copy in group:
             copy.wait_send()
-    for store in stores:
-        store.wait()
 
 
 def body(increment, sea_levels, cell_sigma, level_sigma, diffusivity, band_width, vertical_root):
     nz, rows, columns = increment.shape
     part = nz // CHUNKS
-    vmem = pl.BlockSpec(memory_space=pltpu.VMEM)
     result = pl.pallas_call(
         kernel,
-        out_shape=jax.ShapeDtypeStruct((nz * rows, columns), F32),
+        out_shape=jax.ShapeDtypeStruct((2 * nz * rows, 128), F32),
         in_specs=[
-            pl.BlockSpec(memory_space=pltpu.SMEM),
-            pl.BlockSpec(memory_space=pl.ANY),
-            vmem, vmem, vmem, vmem, vmem,
-        ],
-        out_specs=pl.BlockSpec(memory_space=pl.ANY),
+            pl.BlockSpec(memory_space=pl.ANY)
+        ]
+        * 7,
+        out_specs=pl.BlockSpec(memory_space=pltpu.VMEM),
         scratch_shapes=[
-            pltpu.VMEM((2, nz * rows, 128), F32),
+            pltpu.SMEM(band_width.shape, jnp.int32),
+            pltpu.VMEM(sea_levels.shape, jnp.int32),
+            pltpu.VMEM(cell_sigma.shape, F32),
+            pltpu.VMEM((1, nz), F32),
+            pltpu.VMEM(diffusivity.shape, F32),
+            pltpu.VMEM(vertical_root.shape, F32),
             pltpu.VMEM((2, nz * rows, 128), F32),
             pltpu.VMEM((CHUNKS, 16, part, columns), F32),
             pltpu.VMEM((CHUNKS, 16, part, columns), F32),
             pltpu.VMEM((8, nz, columns), F32),
             pltpu.VMEM((8, nz, columns), F32),
             pltpu.VMEM((2, nz, 128), F32),
-            pltpu.VMEM((2, 3, nz, 128), F32),
+            pltpu.VMEM((2, 2, nz // 2, 128), F32),
+            pltpu.VMEM((2, nz, 128), F32),
+            pltpu.VMEM((2, 2, nz // 2, 128), F32),
             pltpu.VMEM((15, nz, 128), F32),
             pltpu.VMEM((8, 512, 256), BF16),
             pltpu.VMEM((8, 512, 256), BF16),
             pltpu.VMEM((8, 256), F32),
+            pltpu.SemaphoreType.DMA((8,)),
             pltpu.SemaphoreType.DMA((2,)),
-            pltpu.SemaphoreType.DMA((2, 3)),
-            pltpu.SemaphoreType.DMA((2, 3)),
+            pltpu.SemaphoreType.DMA((2,)),
+            pltpu.SemaphoreType.DMA((2, 2)),
+            pltpu.SemaphoreType.DMA((2, 2)),
             pltpu.SemaphoreType.DMA((2, CHUNKS, 2)),
             pltpu.SemaphoreType.DMA((2, CHUNKS, 2)),
         ],
-        compiler_params=pltpu.CompilerParams(collective_id=0, has_side_effects=True),
+        compiler_params=pltpu.CompilerParams(collective_id=0, has_side_effects=True, vmem_limit_bytes=24 * 2**20),
         name="covariance",
-    )(
+    )(*(pltpu.with_memory_space_constraint(x, pltpu.HBM) for x in (
         band_width,
         increment.reshape(nz * rows, columns),
         sea_levels,
@@ -271,7 +307,8 @@
         level_sigma.reshape(1, nz),
         diffusivity,
         vertical_root,
-    )
+    )))
+    result = result.reshape(nz, 2, rows, 128).transpose(0, 2, 1, 3)
     return result.reshape(nz, rows, columns)
 
 

time: 30.9 us -> 27.5 us (0.89)
  Pallas kernels: 28.8 us -> 26.6 us
  local copies, waits for them, and re-layouts: 1.87 us -> 0.8 us
    pallas_call x1, Pallas kernels: 28.8 us -> 26.6 us  [body(): pl.pallas_call(kernel, out_shape=jax.ShapeDtypeStruct((2 * nz * rows, 128...]
    unnamed x1, local copies, waits for them, and re-layouts: 1.87 us -> 0.8 us
where the time goes in v2:
time: 27.5 us; the launch traced here: 27.4 us
  Pallas kernels  26.6 us (97%)
  local copies, waits for them, and re-layouts  0.8 us (3%)
    pallas_call x1, Pallas kernels, body(): pl.pallas_call(kernel, out_shape=jax.ShapeDtypeStruct((2 * nz * rows, 128...  26.6 us
    unnamed x1, local copies, waits for them, and re-layouts  0.8 us

profile of v2, /device:TPU:2, one launch (start us, length us, event | category | flops | bytes accessed | tf_op | source)
XLA Modules:
  0.0 27.4 jit_solution(10914292287676444285)
XLA Ops:
  0.0 26.6 %covariance.1 = f32[1024,128]{1,0:T(8,128)S(1)} custom-call(s32[256]{0:T(256)} %band_hbm.1, f32[512,256]{1,0:T(8,128)} %bitcast.8, s32[8,256]{1,0:T(8,128)} %sea_hbm.1, f32[8,256]{1,0:T(8,128)} %cell_hbm.1, f32[1,64]{1,0:T(1,128)} %bitcast.9, f32[64,256]{1,0:T(8,128)} %diff_hbm.1, f32[64,64]{1,0:T(8,128)} %root_hbm.1), custom_call_target="tpu_custom_call" | custom-call | tf_op jit(solution)/shard_map/covariance/pallas_call | solution.py:264
  26.6 0.8 %copy.9 = f32[64,8,256]{2,1,0:T(8,128)} copy(f32[64,8,256]{2,1,0:T(8,128)S(1)} %bitcast.7) | data formatting | bytes 1048576

commit v3 on v2

--- a/solution.py
+++ b/solution.py
@@ -40,7 +40,7 @@
 def kernel(
     band_hbm, inc_hbm, sea_hbm, cell_hbm, sigma_hbm, diff_hbm, root_hbm, out_ref,
     band_ref, sea_ref, cell_ref, sigma_ref, diff_ref, root_ref,
-    inc_ref, first, second, mid, fin, edge, corner, halo, other, faces_ref, w_high, w_low, zscale,
+    inc_ref, first, second, mid, fin, edge, halo, other, faces_ref, w_high, w_low, zscale,
     load_sem, send_edge, recv_edge, send_corner, recv_corner, send_lat, recv_lat,
 ):
     nz = root_ref.shape[0]
@@ -93,28 +93,24 @@
         high, low = split(start)
         lifted = dot(lift3, jnp.concatenate([high, low, high], axis=0))
         for c in range(CHUNKS):
-            first[c, 4 + j] = lifted[c * part : (c + 1) * part]
+            first[c, 8 + j] = lifted[c * part : (c + 1) * part]
         mine = (lane128 >= HALO * j) & (lane128 < HALO * (j + 1))
         left = pltpu.roll(lifted[:, :128], HALO * j, 1) if j else lifted[:, :128]
         shift = (HALO * j - 112) % 128
         right = pltpu.roll(lifted[:, 128:], shift, 1) if shift else lifted[:, 128:]
         left_pack = jnp.where(mine, left, left_pack)
         right_pack = jnp.where(mine, right, right_pack)
-    low_lanes = lane128[: nz // 2] < 64
-    for side, pack in enumerate((left_pack, right_pack)):
-        edge[side] = pack
-        upper, turned = pack[: nz // 2], pltpu.roll(pack[nz // 2 :], 64, 1)
-        corner[side, 0] = jnp.where(low_lanes, upper, turned)
-        corner[side, 1] = jnp.where(low_lanes, turned, upper)
-
-    def lat_copies(buffer, turn, c):
+    edge[0] = left_pack
+    edge[1] = right_pack
+
+    def lat_copies(c):
         copies = []
-        for way, source, target, a in ((0, 4, 12, south), (1, 8, 0, north)):
+        for way, target, a in ((0, 0, north), (1, 16, south)):
             copy = pltpu.make_async_remote_copy(
-                src_ref=buffer.at[c, pl.ds(source, 4)],
-                dst_ref=buffer.at[c, pl.ds(target, 4)],
-                send_sem=send_lat.at[turn, c, way],
-                recv_sem=recv_lat.at[turn, c, way],
+                src_ref=first.at[c, pl.ds(8, 8)],
+                dst_ref=first.at[c, pl.ds(target, 8)],
+                send_sem=send_lat.at[c, way],
+                recv_sem=recv_lat.at[c, way],
                 device_id={"lat": a, "lon": lon},
                 device_id_type=MESH,
             )
@@ -135,11 +131,11 @@
         )
         copy.start()
         edge_copies.append(copy)
-    first_copies = [lat_copies(first, 0, 0)]
+    first_copies = [lat_copies(0)]
     for side, o in ((0, west), (1, east)):
         for way, a in ((0, south), (1, north)):
             copy = pltpu.make_async_remote_copy(
-                src_ref=corner.at[side, way],
+                src_ref=edge.at[side],
                 dst_ref=other.at[1 - side, way],
                 send_sem=send_corner.at[side, way],
                 recv_sem=recv_corner.at[1 - side, way],
@@ -148,20 +144,20 @@
             )
             copy.start()
             edge_copies.append(copy)
-    first_copies += [lat_copies(first, 0, c) for c in range(1, CHUNKS)]
+    first_copies += [lat_copies(c) for c in range(1, CHUNKS)]
 
     for load in loads[6:]:
         load.wait()
-    column = lax.broadcasted_iota(jnp.int32, (lat_total, 256), 0)
-    block = lax.broadcasted_iota(jnp.int32, (lat_total, 256), 1) // HALO
-    row = 8 * lat + jnp.where(block < 12, block, block - 16)
+    column = lax.broadcasted_iota(jnp.int32, (lat_total, 384), 0)
+    block = lax.broadcasted_iota(jnp.int32, (lat_total, 384), 1) // HALO
+    row = 8 * lat + jnp.where(block < 16, block, block - 24)
     pick = jnp.where((column == row) & (column < lat_total - 1), 1.0, 0.0).astype(BF16)
     d_high, rest = diff_ref[...].astype(BF16), None
     rest = diff_ref[...] - d_high.astype(F32)
     d_mid, d_low = split(rest)
     packed_faces = dot(d_high, pick) + dot(d_mid, pick) + dot(d_low, pick)
-    for m in range(15):
-        lane = HALO * ((m - 4) % 16)
+    for m in range(23):
+        lane = HALO * ((m - 8) % 24)
         faces_ref[m] = jnp.broadcast_to(packed_faces[:, lane : lane + 1], (nz, 128))
 
     inner = (
@@ -172,77 +168,74 @@
     ).astype(F32)
     w_high[...] = jnp.zeros_like(w_high)
     w_low[...] = jnp.zeros_like(w_low)
-    for j in range(8):
-        width = band_ref[8 * lat + j].astype(F32) + 1.0
-        zscale[j : j + 1, :] = 1.0 / jnp.full((1, 256), 6.0 * (width * width) * (width * width), F32)
+    for q in range(16):
+        j = (q - 4) % 8
+        width = band_ref[lax.rem(8 * lat + (q - 4 + lat_total), lat_total)].astype(F32) + 1.0
+        zscale[q : q + 1, :] = 1.0 / jnp.full((1, 256), 6.0 * (width * width) * (width * width), F32)
         for ref, a, b, c in zip(
             (w_high, w_low),
             split(band(inner, width)),
             split(band(outer - 16.0, width)),
             split(band(outer + 128.0, width)),
         ):
-            ref[j, 0:128, 0:128] = a
-            ref[j, 128:256, 128:256] = a
-            ref[j, 112:128, 128:256] = b
-            ref[j, 256 + HALO * j : 272 + HALO * j, 0:128] = b
-            ref[j, 128:144, 0:128] = c
-            ref[j, 384 + HALO * j : 400 + HALO * j, 128:256] = c
+            ref[q, 0:128, 0:128] = a
+            ref[q, 128:256, 128:256] = a
+            ref[q, 112:128, 128:256] = b
+            ref[q, 256 + HALO * j : 272 + HALO * j, 0:128] = b
+            ref[q, 128:144, 0:128] = c
+            ref[q, 384 + HALO * j : 400 + HALO * j, 128:256] = c
 
     def halo_pass():
         for copy in edge_copies:
             copy.wait_recv()
         sides = []
         for side in range(2):
-            above, below = other[side, 0], other[side, 1]
-            far = jnp.concatenate(
-                [
-                    jnp.where(low_lanes, above, below),
-                    pltpu.roll(jnp.where(low_lanes, below, above), 64, 1),
-                ],
-                axis=0,
-            )
-            field = jnp.concatenate([halo[side], far], axis=1)
+            field = jnp.concatenate([halo[side], other[side, 0], other[side, 1]], axis=1)
             for step in range(STEPS):
-                flux = packed_faces * (pltpu.roll(field, 256 - HALO, 1) - field)
+                flux = packed_faces * (pltpu.roll(field, 384 - HALO, 1) - field)
                 field = field + (flux - pltpu.roll(flux, HALO, 1))
-            sides.append(field[:, :128])
-        return split(jnp.concatenate(sides, axis=1))
-
-    def rows_pass(buffer, c, store):
+            sides.append(field)
+        return [
+            split(jnp.concatenate([field[:, 128 * v : 128 * v + 128] for field in sides], axis=1))
+            for v in range(3)
+        ]
+
+    def rows_pass(buffer, c, base, face, store, offset):
         def group(g, carry):
             at = pl.multiple_of(g * 8, 8)
             whole = pl.multiple_of(c * part + g * 8, 8)
-            faces = [faces_ref[m, pl.ds(whole, 8), :] for m in range(15)]
+            faces = [faces_ref[face + m, pl.ds(whole, 8), :] for m in range(15)]
             for half in range(2):
                 lanes = slice(128 * half, 128 * half + 128)
-                rows = [buffer[c, m, pl.ds(at, 8), lanes] for m in range(16)]
+                rows = [buffer[c, base + m, pl.ds(at, 8), lanes] for m in range(16)]
                 for j, value in enumerate(diffuse(rows, faces)):
-                    store[j, pl.ds(whole, 8), lanes] = value
+                    store[offset + j, pl.ds(whole, 8), lanes] = value
             return carry
 
         lax.fori_loop(0, part // 8, group, 0)
 
-    second_copies = []
-    for c in range(CHUNKS):
-        for copy in first_copies[c]:
-            copy.wait_recv()
-        rows_pass(first, c, mid)
-        if c == 0:
-            halo_high, halo_low = halo_pass()
+    def zonal(c, start):
         levels = slice(c * part, (c + 1) * part)
-        for j in range(8):
-            high, low = split(mid[j, levels, :])
+        for q in range(start, start + 8):
+            halo_high, halo_low = halos[0 if 4 <= q < 12 else 1 if q >= 12 else 2]
+            high, low = split(mid[q, levels, :])
             high = jnp.concatenate([high, halo_high[levels]], axis=1)
             low = jnp.concatenate([low, halo_low[levels]], axis=1)
-            both = dot(jnp.concatenate([high, low], axis=0), w_high[j])
-            total = both[:part] + both[part:] + dot(high, w_low[j])
-            second[c, 4 + j] = total * zscale[j : j + 1, :]
-        second_copies.append(lat_copies(second, 1, c))
+            both = dot(jnp.concatenate([high, low], axis=0), w_high[q])
+            total = both[:part] + both[part:] + dot(high, w_low[q])
+            second[c, q] = total * zscale[q : q + 1, :]
 
     for c in range(CHUNKS):
-        for copy in second_copies[c]:
-            copy.wait_recv()
-        rows_pass(second, c, fin)
+        first_copies[c][1].wait_recv()
+        rows_pass(first, c, 8, 8, mid, 8)
+    halos = halo_pass()
+    for c in range(CHUNKS):
+        zonal(c, 8)
+    for c in range(CHUNKS):
+        first_copies[c][0].wait_recv()
+        rows_pass(first, c, 0, 0, mid, 0)
+        zonal(c, 0)
+        rows_pass(second, c, 0, 4, fin, 0)
 
     for j in range(8):
         high, low = split(fin[j])
@@ -253,7 +246,7 @@
             out_ref[pl.ds(8 * h + j, nz, stride=16), :] = result[:, 128 * h : 128 * h + 128]
     for copy in edge_copies:
         copy.wait_send()
-    for group in first_copies + second_copies:
+    for group in first_copies:
         for copy in group:
             copy.wait_send()
 
@@ -277,25 +270,24 @@
             pltpu.VMEM(diffusivity.shape, F32),
             pltpu.VMEM(vertical_root.shape, F32),
             pltpu.VMEM((2, nz * rows, 128), F32),
+            pltpu.VMEM((CHUNKS, 24, part, columns), F32),
             pltpu.VMEM((CHUNKS, 16, part, columns), F32),
-            pltpu.VMEM((CHUNKS, 16, part, columns), F32),
-            pltpu.VMEM((8, nz, columns), F32),
+            pltpu.VMEM((16, nz, columns), F32),
             pltpu.VMEM((8, nz, columns), F32),
             pltpu.VMEM((2, nz, 128), F32),
-            pltpu.VMEM((2, 2, nz // 2, 128), F32),
             pltpu.VMEM((2, nz, 128), F32),
-            pltpu.VMEM((2, 2, nz // 2, 128), F32),
-            pltpu.VMEM((15, nz, 128), F32),
-            pltpu.VMEM((8, 512, 256), BF16),
-            pltpu.VMEM((8, 512, 256), BF16),
-            pltpu.VMEM((8, 256), F32),
+            pltpu.VMEM((2, 2, nz, 128), F32),
+            pltpu.VMEM((23, nz, 128), F32),
+            pltpu.VMEM((16, 512, 256), BF16),
+            pltpu.VMEM((16, 512, 256), BF16),
+            pltpu.VMEM((16, 256), F32),
             pltpu.SemaphoreType.DMA((8,)),
             pltpu.SemaphoreType.DMA((2,)),
             pltpu.SemaphoreType.DMA((2,)),
             pltpu.SemaphoreType.DMA((2, 2)),
             pltpu.SemaphoreType.DMA((2, 2)),
-            pltpu.SemaphoreType.DMA((2, CHUNKS, 2)),
-            pltpu.SemaphoreType.DMA((2, CHUNKS, 2)),
+            pltpu.SemaphoreType.DMA((CHUNKS, 2)),
+            pltpu.SemaphoreType.DMA((CHUNKS, 2)),
         ],
         compiler_params=pltpu.CompilerParams(collective_id=0, has_side_effects=True, vmem_limit_bytes=24 * 2**20),
         name="covariance",

time: 27.5 us -> 26.6 us (0.967)
  the two profiles are of different devices: /device:TPU:2 before, /device:TPU:1 now
where the time goes in v3:
time: 26.6 us; the launch traced here: 26.4 us
  Pallas kernels  25.6 us (96%)
  local copies, waits for them, and re-layouts  0.8 us (3%)
    pallas_call x1, Pallas kernels, body(): pl.pallas_call(kernel, out_shape=jax.ShapeDtypeStruct((2 * nz * rows, 128...  25.6 us
    unnamed x1, local copies, waits for them, and re-layouts  0.8 us

profile of v3, /device:TPU:1, one launch (start us, length us, event | category | flops | bytes accessed | tf_op | source)
XLA Modules:
  0.0 26.4 jit_solution(13737483765142169366)
XLA Ops:
  0.0 25.6 %covariance.1 = f32[1024,128]{1,0:T(8,128)S(1)} custom-call(s32[256]{0:T(256)} %band_hbm.1, f32[512,256]{1,0:T(8,128)} %bitcast.8, s32[8,256]{1,0:T(8,128)} %sea_hbm.1, f32[8,256]{1,0:T(8,128)} %cell_hbm.1, f32[1,64]{1,0:T(1,128)} %bitcast.9, f32[64,256]{1,0:T(8,128)} %diff_hbm.1, f32[64,64]{1,0:T(8,128)} %root_hbm.1), custom_call_target="tpu_custom_call" | custom-call | tf_op jit(solution)/shard_map/covariance/pallas_call | solution.py:257
  25.6 0.8 %copy.9 = f32[64,8,256]{2,1,0:T(8,128)} copy(f32[64,8,256]{2,1,0:T(8,128)S(1)} %bitcast.7) | data formatting | bytes 1048576

commit v4 on v3

--- a/solution.py
+++ b/solution.py
@@ -40,7 +40,7 @@
 def kernel(
     band_hbm, inc_hbm, sea_hbm, cell_hbm, sigma_hbm, diff_hbm, root_hbm, out_ref,
     band_ref, sea_ref, cell_ref, sigma_ref, diff_ref, root_ref,
-    inc_ref, first, second, mid, fin, edge, halo, other, faces_ref, w_high, w_low, zscale,
+    inc_ref, first, second, mid, fin, edge, halo, other, faces_ref, w_high, w_low, zscale, halos,
     load_sem, send_edge, recv_edge, send_corner, recv_corner, send_lat, recv_lat,
 ):
     nz = root_ref.shape[0]
@@ -64,12 +64,16 @@
         loads.append(pltpu.make_async_copy(source, target, load_sem.at[2 + i]))
     for load in loads:
         load.start()
+    has_south, has_north = lat > 0, lat < lat_count - 1
     barrier = pltpu.get_barrier_semaphore()
-    for a, o in (
-        (north, lon), (south, lon), (lat, east), (lat, west),
-        (north, east), (north, west), (south, east), (south, west),
-    ):
-        pl.semaphore_signal(barrier, inc=1, device_id={"lat": a, "lon": o}, device_id_type=MESH)
+
+    def greet(a, columns):
+        for o in columns:
+            pl.semaphore_signal(barrier, inc=1, device_id={"lat": a, "lon": o}, device_id_type=MESH)
+
+    greet(lat, (east, west))
+    pl.when(has_south)(lambda: greet(south, (lon, east, west)))
+    pl.when(has_north)(lambda: greet(north, (lon, east, west)))
 
     loads[2].wait()
     loads[3].wait()
@@ -103,22 +107,32 @@
     edge[0] = left_pack
     edge[1] = right_pack
 
-    def lat_copies(c):
-        copies = []
-        for way, target, a in ((0, 0, north), (1, 16, south)):
-            copy = pltpu.make_async_remote_copy(
-                src_ref=first.at[c, pl.ds(8, 8)],
-                dst_ref=first.at[c, pl.ds(target, 8)],
-                send_sem=send_lat.at[c, way],
-                recv_sem=recv_lat.at[c, way],
-                device_id={"lat": a, "lon": lon},
-                device_id_type=MESH,
-            )
-            copy.start()
-            copies.append(copy)
-        return copies
-
-    pl.semaphore_wait(barrier, 8)
+    @pl.when(jnp.logical_not(has_south))
+    def _():
+        first[:, 0:8] = jnp.zeros_like(first[:, 0:8])
+        other[:, 1] = jnp.zeros_like(other[:, 1])
+
+    @pl.when(jnp.logical_not(has_north))
+    def _():
+        first[:, 16:24] = jnp.zeros_like(first[:, 16:24])
+        other[:, 0] = jnp.zeros_like(other[:, 0])
+
+    def lat_copy(c, way, a):
+        return pltpu.make_async_remote_copy(
+            src_ref=first.at[c, pl.ds(8, 8)],
+            dst_ref=first.at[c, pl.ds(16 * way, 8)],
+            send_sem=send_lat.at[c, way],
+            recv_sem=recv_lat.at[c, way],
+            device_id={"lat": a, "lon": lon},
+            device_id_type=MESH,
+        )
+
+    def send_rows(c):
+        pl.when(has_north)(lambda: lat_copy(c, 0, north).start())
+        pl.when(has_south)(lambda: lat_copy(c, 1, south).start())
+
+    inside = has_south.astype(jnp.int32) + has_north.astype(jnp.int32)
+    pl.semaphore_wait(barrier, 2 + 3 * inside)
     edge_copies = []
     for side, o in ((0, west), (1, east)):
         copy = pltpu.make_async_remote_copy(
@@ -131,10 +145,10 @@
         )
         copy.start()
         edge_copies.append(copy)
-    first_copies = [lat_copies(0)]
-    for side, o in ((0, west), (1, east)):
-        for way, a in ((0, south), (1, north)):
-            copy = pltpu.make_async_remote_copy(
+    send_rows(0)
+    def corner_copies(way, a):
+        return [
+            pltpu.make_async_remote_copy(
                 src_ref=edge.at[side],
                 dst_ref=other.at[1 - side, way],
                 send_sem=send_corner.at[side, way],
@@ -142,9 +156,17 @@
                 device_id={"lat": a, "lon": o},
                 device_id_type=MESH,
             )
-            copy.start()
-            edge_copies.append(copy)
-    first_copies += [lat_copies(c) for c in range(1, CHUNKS)]
+            for side, o in ((0, west), (1, east))
+        ]
+
+    def each(copies, action):
+        for copy in copies:
+            getattr(copy, action)()
+
+    pl.when(has_south)(lambda: each(corner_copies(0, south), "start"))
+    pl.when(has_north)(lambda: each(corner_copies(1, north), "start"))
+    for c in range(1, CHUNKS):
+        send_rows(c)
 
     for load in loads[6:]:
         load.wait()
@@ -171,7 +193,7 @@
     for q in range(16):
         j = (q - 4) % 8
         width = band_ref[lax.rem(8 * lat + (q - 4 + lat_total), lat_total)].astype(F32) + 1.0
-        zscale[q : q + 1, :] = 1.0 / jnp.full((1, 256), 6.0 * (width * width) * (width * width), F32)
+        zscale[q] = 1.0 / jnp.full((1, 256), 6.0 * (width * width) * (width * width), F32)
         for ref, a, b, c in zip(
             (w_high, w_low),
             split(band(inner, width)),
@@ -186,8 +208,9 @@
             ref[q, 384 + HALO * j : 400 + HALO * j, 128:256] = c
 
     def halo_pass():
-        for copy in edge_copies:
-            copy.wait_recv()
+        each(edge_copies, "wait_recv")
+        pl.when(has_north)(lambda: each(corner_copies(0, south), "wait_recv"))
+        pl.when(has_south)(lambda: each(corner_copies(1, north), "wait_recv"))
         sides = []
         for side in range(2):
             field = jnp.concatenate([halo[side], other[side, 0], other[side, 1]], axis=1)
@@ -195,10 +218,10 @@
                 flux = packed_faces * (pltpu.roll(field, 384 - HALO, 1) - field)
                 field = field + (flux - pltpu.roll(flux, HALO, 1))
             sides.append(field)
-        return [
-            split(jnp.concatenate([field[:, 128 * v : 128 * v + 128] for field in sides], axis=1))
-            for v in range(3)
-        ]
+        for v in range(3):
+            halos[v, 0], halos[v, 1] = split(
+                jnp.concatenate([field[:, 128 * v : 128 * v + 128] for field in sides], axis=1)
+            )
 
     def rows_pass(buffer, c, base, face, store, offset):
         def group(g, carry):
@@ -214,27 +237,33 @@
 
         lax.fori_loop(0, part // 8, group, 0)
 
-    def zonal(c, start):
+    def zonal(c, half):
         levels = slice(c * part, (c + 1) * part)
-        for q in range(start, start + 8):
-            halo_high, halo_low = halos[0 if 4 <= q < 12 else 1 if q >= 12 else 2]
+        for i in range(8):
+            q = 8 * half + i
+            group = 2 - 2 * half if i < 4 else half
             high, low = split(mid[q, levels, :])
-            high = jnp.concatenate([high, halo_high[levels]], axis=1)
-            low = jnp.concatenate([low, halo_low[levels]], axis=1)
+            high = jnp.concatenate([high, halos[group, 0, levels, :]], axis=1)
+            low = jnp.concatenate([low, halos[group, 1, levels, :]], axis=1)
             both = dot(jnp.concatenate([high, low], axis=0), w_high[q])
             total = both[:part] + both[part:] + dot(high, w_low[q])
-            second[c, q] = total * zscale[q : q + 1, :]
-
+            second[c, q] = total * zscale[q]
+
+    def receive(c, half):
+        there = jnp.where(half == 0, lat, lat_count - 1 - lat) > 0
+        pl.when(there)(lambda: lat_copy(c, half, north).wait_recv())
+        rows_pass(first, c, 8 * half, 8 * half, mid, 8 * half)
+
+    late = lax.rem(lat, 2)
+    early = 1 - late
     for c in range(CHUNKS):
-        first_copies[c][1].wait_recv()
-        rows_pass(first, c, 8, 8, mid, 8)
-    halos = halo_pass()
+        receive(c, early)
+    halo_pass()
     for c in range(CHUNKS):
-        zonal(c, 8)
+        zonal(c, early)
     for c in range(CHUNKS):
-        first_copies[c][0].wait_recv()
-        rows_pass(first, c, 0, 0, mid, 0)
-        zonal(c, 0)
+        receive(c, late)
+        zonal(c, late)
         rows_pass(second, c, 0, 4, fin, 0)
 
     for j in range(8):
@@ -244,11 +273,14 @@
         result = jnp.where(sea, lowered * cell_ref[j : j + 1, :], 0.0)
         for h in range(2):
             out_ref[pl.ds(8 * h + j, nz, stride=16), :] = result[:, 128 * h : 128 * h + 128]
-    for copy in edge_copies:
-        copy.wait_send()
-    for group in first_copies:
-        for copy in group:
-            copy.wait_send()
+    each(edge_copies, "wait_send")
+
+    def sent(corner_way, a, way):
+        each(corner_copies(corner_way, a), "wait_send")
+        each([lat_copy(c, way, a) for c in range(CHUNKS)], "wait_send")
+
+    pl.when(has_south)(lambda: sent(0, south, 1))
+    pl.when(has_north)(lambda: sent(1, north, 0))
 
 
 def body(increment, sea_levels, cell_sigma, level_sigma, diffusivity, band_width, vertical_root):
@@ -280,7 +312,8 @@
             pltpu.VMEM((23, nz, 128), F32),
             pltpu.VMEM((16, 512, 256), BF16),
             pltpu.VMEM((16, 512, 256), BF16),
-            pltpu.VMEM((16, 256), F32),
+            pltpu.VMEM((16, 1, 256), F32),
+            pltpu.VMEM((3, 2, nz, columns), BF16),
             pltpu.SemaphoreType.DMA((8,)),
             pltpu.SemaphoreType.DMA((2,)),
             pltpu.SemaphoreType.DMA((2,)),

time: 26.6 us -> 25.5 us (0.959)
  the two profiles are of different devices: /device:TPU:1 before, /device:TPU:2 now
where the time goes in v4:
time: 25.5 us; the launch traced here: 25.3 us
  Pallas kernels  24.5 us (96%)
  local copies, waits for them, and re-layouts  0.8 us (3%)
    pallas_call x1, Pallas kernels, body(): pl.pallas_call(kernel, out_shape=jax.ShapeDtypeStruct((2 * nz * rows, 128...  24.5 us
    unnamed x1, local copies, waits for them, and re-layouts  0.8 us

profile of v4, /device:TPU:2, one launch (start us, length us, event | category | flops | bytes accessed | tf_op | source)
XLA Modules:
  0.0 25.3 jit_solution(2127151042209085188)
XLA Ops:
  0.0 24.5 %covariance.1 = f32[1024,128]{1,0:T(8,128)S(1)} custom-call(s32[256]{0:T(256)} %band_hbm.1, f32[512,256]{1,0:T(8,128)} %bitcast.8, s32[8,256]{1,0:T(8,128)} %sea_hbm.1, f32[8,256]{1,0:T(8,128)} %cell_hbm.1, f32[1,64]{1,0:T(1,128)} %bitcast.9, f32[64,256]{1,0:T(8,128)} %diff_hbm.1, f32[64,64]{1,0:T(8,128)} %root_hbm.1), custom_call_target="tpu_custom_call" | custom-call | tf_op jit(solution)/shard_map/covariance/pallas_call | solution.py:289
  24.5 0.8 %copy.9 = f32[64,8,256]{2,1,0:T(8,128)} copy(f32[64,8,256]{2,1,0:T(8,128)S(1)} %bitcast.7) | data formatting | bytes 1048576

commit v5 on v4

--- a/solution.py
+++ b/solution.py
@@ -40,7 +40,7 @@
 def kernel(
     band_hbm, inc_hbm, sea_hbm, cell_hbm, sigma_hbm, diff_hbm, root_hbm, out_ref,
     band_ref, sea_ref, cell_ref, sigma_ref, diff_ref, root_ref,
-    inc_ref, first, second, mid, fin, edge, halo, other, faces_ref, w_high, w_low, zscale, halos,
+    inc_ref, first, second, mid, fin, edge, halo, other, faces_ref, w_high, w_low, zscale, halos, sums,
     load_sem, send_edge, recv_edge, send_corner, recv_corner, send_lat, recv_lat,
 ):
     nz = root_ref.shape[0]
@@ -81,7 +81,10 @@
     lift_high, lift_low = split(lift)
     lift3 = jnp.concatenate([lift_high, lift_high, lift_low], axis=1)
     lower_high, lower_low = split(lift.T)
-    lower3 = jnp.concatenate([lower_high, lower_high, lower_low], axis=1)
+    lower3 = []
+    for c in range(CHUNKS):
+        high, low = (x[:, c * part : (c + 1) * part] for x in (lower_high, lower_low))
+        lower3.append(jnp.concatenate([high, high, low], axis=1))
 
     level = lax.broadcasted_iota(jnp.int32, (nz, 256), 0)
     lane128 = lax.broadcasted_iota(jnp.int32, (nz, 128), 1)
@@ -145,7 +148,6 @@
         )
         copy.start()
         edge_copies.append(copy)
-    send_rows(0)
     def corner_copies(way, a):
         return [
             pltpu.make_async_remote_copy(
@@ -165,7 +167,7 @@
 
     pl.when(has_south)(lambda: each(corner_copies(0, south), "start"))
     pl.when(has_north)(lambda: each(corner_copies(1, north), "start"))
-    for c in range(1, CHUNKS):
+    for c in range(CHUNKS):
         send_rows(c)
 
     for load in loads[6:]:
@@ -235,7 +237,7 @@
                     store[offset + j, pl.ds(whole, 8), lanes] = value
             return carry
 
-        lax.fori_loop(0, part // 8, group, 0)
+        lax.fori_loop(0, part // 8, group, 0, unroll=True)
 
     def zonal(c, half):
         levels = slice(c * part, (c + 1) * part)
@@ -265,14 +267,19 @@
         receive(c, late)
         zonal(c, late)
         rows_pass(second, c, 0, 4, fin, 0)
-
-    for j in range(8):
-        high, low = split(fin[j])
-        lowered = dot(lower3, jnp.concatenate([high, low, high], axis=0))
-        sea = level < sea_ref[j : j + 1, :]
-        result = jnp.where(sea, lowered * cell_ref[j : j + 1, :], 0.0)
-        for h in range(2):
-            out_ref[pl.ds(8 * h + j, nz, stride=16), :] = result[:, 128 * h : 128 * h + 128]
+        for j in range(8):
+            high, low = split(fin[j, c * part : (c + 1) * part, :])
+            lowered = dot(lower3[c], jnp.concatenate([high, low, high], axis=0))
+            if c:
+                lowered = lowered + sums[j]
+            if c < CHUNKS - 1:
+                sums[j] = lowered
+                continue
+            sea = level < sea_ref[j : j + 1, :]
+            result = jnp.where(sea, lowered * cell_ref[j : j + 1, :], 0.0)
+            for h in range(2):
+                out_ref[pl.ds(8 * h + j, nz, stride=16), :] = result[:, 128 * h : 128 * h + 128]
+
     each(edge_copies, "wait_send")
 
     def sent(corner_way, a, way):
@@ -314,6 +321,7 @@
             pltpu.VMEM((16, 512, 256), BF16),
             pltpu.VMEM((16, 1, 256), F32),
             pltpu.VMEM((3, 2, nz, columns), BF16),
+            pltpu.VMEM((8, nz, columns), F32),
             pltpu.SemaphoreType.DMA((8,)),
             pltpu.SemaphoreType.DMA((2,)),
             pltpu.SemaphoreType.DMA((2,)),

time: 25.5 us -> 25.1 us (0.984)
  Pallas kernels: 24.5 us -> 24.2 us
    pallas_call x1, Pallas kernels: 24.5 us -> 24.2 us  [body(): pl.pallas_call(kernel, out_shape=jax.ShapeDtypeStruct((2 * nz * rows, 128...]
where the time goes in v5:
time: 25.1 us; the launch traced here: 25 us
  Pallas kernels  24.2 us (96%)
  local copies, waits for them, and re-layouts  0.8 us (3%)
    pallas_call x1, Pallas kernels, body(): pl.pallas_call(kernel, out_shape=jax.ShapeDtypeStruct((2 * nz * rows, 128...  24.2 us
    unnamed x1, local copies, waits for them, and re-layouts  0.8 us

profile of v5, /device:TPU:2, one launch (start us, length us, event | category | flops | bytes accessed | tf_op | source)
XLA Modules:
  0.0 25.0 jit_solution(3174628584220516151)
XLA Ops:
  0.0 24.2 %covariance.1 = f32[1024,128]{1,0:T(8,128)S(1)} custom-call(s32[256]{0:T(256)} %band_hbm.1, f32[512,256]{1,0:T(8,128)} %bitcast.8, s32[8,256]{1,0:T(8,128)} %sea_hbm.1, f32[8,256]{1,0:T(8,128)} %cell_hbm.1, f32[1,64]{1,0:T(1,128)} %bitcast.9, f32[64,256]{1,0:T(8,128)} %diff_hbm.1, f32[64,64]{1,0:T(8,128)} %root_hbm.1), custom_call_target="tpu_custom_call" | custom-call | tf_op jit(solution)/shard_map/covariance/pallas_call | solution.py:296
  24.2 0.8 %copy.9 = f32[64,8,256]{2,1,0:T(8,128)} copy(f32[64,8,256]{2,1,0:T(8,128)S(1)} %bitcast.7) | data formatting | bytes 1048576
